TPU v7x, 128 devices: a whole 4x4x4 slice. The times are simulated.
128 devices in a mesh: sess: 32 (over x, z, core), tp: 4 (over y).
Axes of the slice: x: 4, y: 4, z: 4, core: 2. Of those that a mesh axis runs over, the one named last changes fastest.
Arguments:
- hidden: bfloat16 [16384, 8192], P('sess'), may hold values from -6 to 6
- routes: int32 [16384, 1], replicated, may hold values from 0 to 63; in each aligned block of 512 rows (0 to 511, 512 to 1023, ...) at most 16 rows name the same one
- w_qkv: bfloat16 [8192, 4, 1280], P(None, 'tp'), may hold values from -0.0625 to 0.0625
- b_qkv: float32 [4, 1280], P('tp'), may hold values from -8 to 8
- pool: bfloat16 [512, 4, 64, 256], P('sess', 'tp'), may hold values from -8 to 8
- page_lists: int32 [64, 4, 8], replicated, may hold values from 0 to 511, as said below
Outputs:
- attn_out: bfloat16 [64, 512, 4096], P('sess', None, 'tp')
Inputs may be any that keep to these rules, and one draw needn't show every extreme that they name: `routes`: within the rows of one ingest index no session is named by more than 16 rows, a bound that some block reaches. `page_lists`: page p lies on pool index p // 16. For the sessions of one owner (sessions o * 2 to o * 2 + 1) and one 4 head, the 16 listed pages lie on distinct pool indices, exactly 1 on each of them.
All inputs are finite; a program needn't handle non-finite values.
Results may differ from a plain program's by a relative error of at most 0.0065.
Values may be sent and summed in bfloat16 or wider, within the bound.
A program may use at most 192 MiB of HBM per device.

v0:
```python
import math

import jax
import jax.numpy as jnp
from jax import lax
from jax.sharding import PartitionSpec as P

HD = 128
QPK = 8


def place_rows(part_rows, destination, ranking, per_owner, owners, slot_most):
    owner_of = destination // per_owner
    local_of = destination % per_owner
    target = local_of * (owners * slot_most) + owner_of * slot_most + ranking
    buffer = jnp.zeros((per_owner * owners * slot_most, part_rows.shape[1]), part_rows.dtype)
    buffer = buffer.at[target].set(part_rows)
    return buffer.reshape(per_owner, owners * slot_most, part_rows.shape[1])


def on_device(hidden, routes, w_qkv, b_qkv, pool, page_lists):
    owners = lax.axis_size("sess")
    owner_index = lax.axis_index("sess")
    head_index = lax.axis_index("tp")
    rows_here = hidden.shape[0]
    sessions = page_lists.shape[0]
    per_owner = sessions // owners
    slot_most = 2 * rows_here // sessions
    segment = owners * slot_most
    weights = w_qkv[:, 0, :]
    bias = b_qkv[0]
    scale = 1.0 / math.sqrt(HD)
    session_ids = jnp.arange(sessions, dtype=jnp.int32)
    blocks = routes[:, 0].reshape(owners, rows_here)
    destination = lax.dynamic_index_in_dim(blocks, owner_index, 0, keepdims=False)
    onehot = (destination[:, None] == session_ids[None, :]).astype(jnp.int32)
    ranking = jnp.sum(jnp.cumsum(onehot, axis=0) * onehot, axis=1) - 1
    my_sessions = owner_index * per_owner + jnp.arange(per_owner, dtype=jnp.int32)
    counts = jnp.sum((blocks[:, :, None] == my_sessions[None, None, :]).astype(jnp.int32), axis=1)
    starts = jnp.cumsum(counts, axis=0) - counts
    offsets = jnp.arange(slot_most, dtype=jnp.int32)
    live = (offsets[None, None, :] < counts.T[:, :, None]).reshape(per_owner, segment)
    position = (starts.T[:, :, None] + offsets[None, None, :]).reshape(per_owner, segment)
    local_rows = jnp.dot(hidden, weights, preferred_element_type=jnp.float32)
    local_rows = (local_rows + bias).astype(jnp.bfloat16)
    sendable = place_rows(local_rows, destination, ranking, per_owner, owners, slot_most)
    qkv = lax.all_to_all(sendable, "sess", split_axis=1, concat_axis=1, tiled=True)
    pool_dev = pool.shape[0]
    kept = page_lists.shape[2]
    requests = per_owner * kept
    page_cap = max(1, requests // owners)
    lists = lax.dynamic_index_in_dim(page_lists, head_index, 1, keepdims=False).reshape(
        owners, requests
    )
    source_dev = lists // pool_dev
    source_slot = lists % pool_dev
    request_ids = jnp.arange(requests, dtype=jnp.int32)
    before = request_ids[None, :] < request_ids[:, None]
    same_dev = source_dev[:, :, None] == source_dev[:, None, :]
    page_rank = jnp.sum((same_dev & before[None]).astype(jnp.int32), axis=2)
    cap_ids = jnp.arange(page_cap, dtype=jnp.int32)
    matched = (source_dev == owner_index)[:, :, None] & (
        page_rank[:, :, None] == cap_ids[None, None, :]
    )
    slot_pick = jnp.sum(jnp.where(matched, source_slot[:, :, None], 0), axis=1).reshape(
        owners * page_cap
    )
    present = jnp.any(matched, axis=1).reshape(owners * page_cap)
    local_pool = pool[:, 0]
    outgoing = jnp.where(present[:, None, None], local_pool[slot_pick], jnp.zeros((), jnp.bfloat16))
    arrived_pages = lax.all_to_all(outgoing, "sess", split_axis=0, concat_axis=0, tiled=True)
    my_dev = lax.dynamic_index_in_dim(source_dev, owner_index, 0, keepdims=False)
    my_rank = lax.dynamic_index_in_dim(page_rank, owner_index, 0, keepdims=False)
    history = arrived_pages[my_dev * page_cap + my_rank].reshape(
        per_owner, kept * pool.shape[2], pool.shape[3]
    )
    kept_tokens = history.shape[1]
    query_cols = QPK * HD
    query = qkv[:, :, :query_cols].reshape(per_owner, segment, QPK, HD)
    keys = jnp.concatenate([history[:, :, :HD], qkv[:, :, query_cols : query_cols + HD]], axis=1)
    values = jnp.concatenate([history[:, :, HD:], qkv[:, :, query_cols + HD :]], axis=1)
    scores = jnp.einsum("bsgd,bnd->bgsn", query, keys, preferred_element_type=jnp.float32) * scale
    recent = live[:, None, :] & (position[:, None, :] <= position[:, :, None])
    allowed = jnp.concatenate(
        [jnp.ones((per_owner, segment, kept_tokens), jnp.bool_), recent], axis=2
    )[:, None]
    scores = jnp.where(allowed, scores, -1e30)
    top = jnp.max(scores, axis=-1, keepdims=True)
    expo = jnp.where(allowed, jnp.exp(scores - top), 0.0)
    probs = (expo / jnp.sum(expo, axis=-1, keepdims=True)).astype(jnp.bfloat16)
    attended = jnp.einsum("bgsn,bnd->bsgd", probs, values, preferred_element_type=jnp.float32)
    attended = jnp.where(live[:, :, None, None], attended, 0.0)
    return attended.reshape(per_owner, segment, query_cols).astype(jnp.bfloat16)


def solution(mesh):
    in_specs = (
        P("sess", None),
        P(),
        P(None, "tp", None),
        P("tp", None),
        P("sess", "tp", None, None),
        P(),
    )
    out_specs = P("sess", None, "tp")
    return jax.shard_map(
        on_device, mesh=mesh, in_specs=in_specs, out_specs=out_specs, check_vma=False
    )
```

profile of v0, /device:TPU:1, one launch (start us, length us, event | category | flops | bytes accessed | tf_op | source)
XLA Modules:
  0.0 129.8 jit_solution(2608155189427158736)
XLA Ops:
  0.0 0.7 constant_dynamic-slice_fusion.1
  0.8 0.1 copy.88
  0.9 0.1 reshape.358
  0.9 0.1 copy.66
  1.0 0.1 convert_reduce_fusion
  1.2 0.1 copy.70
  1.3 0.1 eq.95
  1.3 0.1 fusion.44
  1.5 0.1 fusion.26
  1.6 0.1 reduce_or.14
  1.7 0.1 reduce_sum.57
  1.8 0.1 reduce_sum.58
  2.0 0.1 reduce_or.18
  2.1 0.6 gather_fusion
  2.7 1.1 broadcast_select_fusion
  3.8 9.5 %all-to-all-start = ((bf16[32,64,256]{2,1,0:T(8,128)(2,1)}), bf16[32,64,256]{2,1,0:T(8,128)(2,1)}, u32[]{:S(2)}, u32[]{:S(2)}) async-start(bf16[32,64,256]{2,1,0:T(8,128)(2,1)} %broadcast_select_fusion), calls=%async_computation | async-start | bytes 2097152 | tf_op jit(solution)/shard_map/all_to_all | solution.py:71
  13.3 0.5 broadcast.377
  13.8 0.8 reduce.14
  14.7 17.6 %fusion.13 = bf16[512,1280]{1,0:T(8,128)(2,1)} fusion(bf16[512,8192]{1,0:T(8,128)(2,1)} %param.6, bf16[8192,1,1280]{2,0,1:T(8,128)(2,1)} %param.8, f32[1280]{0:T(1024)S(1)} %reduce.9), kind=kOutput, calls=%fused_computation.17 | convolution fusion | flops 10738728960 | bytes 30675968 | tf_op jit(solution)/shard_map/dot_general | solution.py:44
  32.3 1.2 reduce-window.6
  33.5 0.2 slice_reduce_fusion
  33.8 0.1 fusion.22
  34.0 4.6 %scatter_custom_fusion = bf16[1024,1280]{1,0:T(8,128)(2,1)S(1)} fusion(s32[512]{0:T(512)S(1)} %bitcast.106, bf16[512,1280]{1,0:T(8,128)(2,1)} %fusion.13, bf16[]{:T(256)} %constant.102.clone.1), kind=kCustom, calls=%fused_computation.19 | custom fusion | bytes 2621952 | tf_op jit(solution)/shard_map/scatter | solution.py:17
  38.6 4.2 %copy.72 = bf16[2,512,1280]{2,0,1:T(2,128)(2,1)} copy(bf16[2,512,1280]{2,1,0:T(8,128)(2,1)S(1)} %bitcast.98) | data formatting | bytes 5242880 | tf_op jit(solution)/shard_map/reshape | solution.py:18
  42.8 0.0 all-to-all-done
  42.8 7.4 %all-to-all-start.1 = ((bf16[2,512,1280]{2,0,1:T(2,128)(2,1)}), bf16[2,512,1280]{2,0,1:T(2,128)(2,1)S(1)}, u32[]{:S(2)}, u32[]{:S(2)}) async-start(bf16[2,512,1280]{2,0,1:T(2,128)(2,1)} %copy.72), calls=%async_computation.1 | async-start | bytes 5242880 | tf_op jit(solution)/shard_map/all_to_all | solution.py:47
  50.2 0.1 lt.108
  50.3 0.2 convert_reduce_fusion.1
  50.5 0.1 copy.63
  50.6 0.1 reduce_window_sum.30
  50.6 0.1 copy.64
  50.7 0.1 copy.75
  50.8 0.1 add.190
  50.9 0.1 add.191
  51.0 0.1 lt.110
  51.0 0.1 lt.111
  51.2 0.5 compare_and_fusion
  51.7 1.3 concatenate.10
  53.0 0.2 add_reduce_fusion
  53.2 1.8 %gather_fusion.1 = bf16[16,64,256]{2,1,0:T(8,128)(2,1)S(1)} fusion(bf16[32,64,256]{2,1,0:T(8,128)(2,1)} %all-to-all-done, s32[1024]{0:T(1024)S(1)} %pad_clamp_fusion), kind=kCustom, calls=%fused_computation.1 | custom fusion | bytes 1048640 | tf_op jit(solution)/shard_map/gather | solution.py:74
  55.0 0.8 fusion.47
  55.8 28.3 %all-to-all-done.1 = bf16[2,512,1280]{2,0,1:T(2,128)(2,1)S(1)} async-done(((bf16[2,512,1280]{2,0,1:T(2,128)(2,1)}), bf16[2,512,1280]{2,0,1:T(2,128)(2,1)S(1)}, u32[]{:S(2)}, u32[]{:S(2)}) %all-to-all-start.1) | async-done | bytes 2621472 | tf_op jit(solution)/shard_map/all_to_all | solution.py:47
  84.1 2.8 %slice.37 = bf16[2,512,1024]{2,0,1:T(2,128)(2,1)} slice(bf16[2,512,1280]{2,0,1:T(2,128)(2,1)S(1)} %all-to-all-done.1), slice={[0:2], [0:512], [0:1024]} | slice | bytes 4194304 | tf_op jit(solution)/shard_map/slice | solution.py:79
  86.8 6.1 %copy.91 = bf16[2,512,1024]{1,2,0:T(8,128)(2,1)} copy(bf16[2,512,1024]{2,0,1:T(2,128)(2,1)} %slice.37) | data formatting | bytes 4194304
  93.0 0.4 fusion.46
  93.4 21.9 %fusion.48 = (f32[2,8,512]{2,1,0:T(8,128)S(1)}, f32[2,8,512,1024]{2,3,1,0:T(8,128)}) fusion(bf16[2,512,8,128]{1,3,2,0:T(8,128)(2,1)} %bitcast.99, pred[2,512,1024]{1,2,0:T(8,128)(4,1)} %concatenate.10, bf16[2,512,128]{2,1,0:T(8,128)(2,1)S(1)} %copy.90, bf16[2,512,128]{2,1,0:T(8,128)(2,1)} %get-tuple-element.10), kind=kOutput, calls=%fused_computation.90 | convolution fusion | flops 2190476288 | bytes 37257216 | tf_op jit(solution)/shard_map/sub | solution.py:89
  115.3 12.1 %select_convert_fusion = bf16[2,128,8,512]{3,1,2,0:T(8,128)(2,1)S(1)} fusion(pred[2,512]{1,0:T(4,128)(4,1)S(1)} %broadcast_compare_fusion.1, f32[2,8,512,1024]{2,3,1,0:T(8,128)} %get-tuple-element.12, f32[2,8,512]{2,1,0:T(8,128)S(1)} %get-tuple-element.11, bf16[2,512,128]{2,1,0:T(8,128)(2,1)S(1)} %copy.89, bf16[2,512,128]{2,1,0:T(8,128)(2,1)S(1)} %get-tuple-element.9), kind=kOutput, calls=%fused_computation.15 | convolution fusion | flops 2167406592 | bytes 36209664 | tf_op jit(solution)/shard_map/bgsn,bnd->bsgd/dot_general | solution.py:91
  127.4 2.4 %copy.81 = bf16[2,512,1024]{2,1,0:T(8,128)(2,1)} copy(bf16[2,512,1024]{1,2,0:T(8,128)(2,1)S(1)} %bitcast.100) | data formatting | bytes 4194304 | tf_op jit(solution)/shard_map/convert_element_type | solution.py:93
  (30 shorter events, 0.3 us)
Async XLA Ops:
  0.0 2.1 %copy-start = (bf16[16,1,64,256]{3,2,1,0:T(8,128)(2,1)S(1)}, bf16[16,1,64,256]{3,2,1,0:T(8,128)(2,1)}, u32[]{:S(2)}) copy-start(bf16[16,1,64,256]{3,2,1,0:T(8,128)(2,1)} %param.10) | copy-start | bytes 1572868
  0.0 13.8 %copy-start.2 = (s32[16384,1]{0,1:T(1,128)S(1)}, s32[16384,1]{0,1:T(1,128)}, u32[]{:S(2)}) copy-start(s32[16384,1]{0,1:T(1,128)} %param.7) | copy-start | bytes 196612
  0.0 14.6 %copy-start.3 = (f32[1,1280]{1,0:T(1,128)S(1)}, f32[1,1280]{1,0:T(1,128)}, u32[]{:S(2)}) copy-start(f32[1,1280]{1,0:T(1,128)} %param.9) | copy-start | bytes 15364
  3.8 39.0 %all-to-all-start = ((bf16[32,64,256]{2,1,0:T(8,128)(2,1)}), bf16[32,64,256]{2,1,0:T(8,128)(2,1)}, u32[]{:S(2)}, u32[]{:S(2)}) async-start(bf16[32,64,256]{2,1,0:T(8,128)(2,1)} %broadcast_select_fusion), calls=%async_computation | async-start | bytes 2097152 | tf_op jit(solution)/shard_map/all_to_all | solution.py:71
  42.8 41.3 %all-to-all-start.1 = ((bf16[2,512,1280]{2,0,1:T(2,128)(2,1)}), bf16[2,512,1280]{2,0,1:T(2,128)(2,1)S(1)}, u32[]{:S(2)}, u32[]{:S(2)}) async-start(bf16[2,512,1280]{2,0,1:T(2,128)(2,1)} %copy.72), calls=%async_computation.1 | async-start | bytes 5242880 | tf_op jit(solution)/shard_map/all_to_all | solution.py:47
  115.3 14.5 %copy-start.1 = (bf16[16,1,64,256]{3,2,1,0:T(8,128)(2,1)S(1)}, bf16[16,1,64,256]{3,2,1,0:T(8,128)(2,1)}, u32[]{:S(2)}) copy-start(bf16[16,1,64,256]{3,2,1,0:T(8,128)(2,1)} %param.10) | copy-start | bytes 1572868
where the time goes:
time: 130 us
  matrix products  51.6 us (40%)
  waiting for transfers between devices  28.3 us (22%)
  local copies, waits for them, and re-layouts  27.8 us (21%)
  starting transfers between devices  16.9 us (13%)
  other arithmetic  4.97 us (4%)
    all_to_all x1, waiting for transfers between devices, on_device(): lax.all_to_all(sendable, 'sess', split_axis=1, concat_axis=1, tiled=True)  28.3 us
    sub x1, matrix products, on_device(): expo = jnp.where(allowed, jnp.exp(scores - top), 0.0)  21.9 us
    dot_general x1, matrix products, on_device(): local_rows = jnp.dot(hidden, weights, preferred_element_type=jnp.float32)  17.6 us
    dot_general x1, matrix products, on_device(): jnp.einsum('bgsn,bnd->bsgd', probs, values, preferred_element_type=jnp.fl...  12.1 us
    all_to_all x1, starting transfers between devices, on_device(): lax.all_to_all(outgoing, 'sess', split_axis=0, concat_axis=0, tiled=True)  9.49 us
    all_to_all x1, starting transfers between devices, on_device(): lax.all_to_all(sendable, 'sess', split_axis=1, concat_axis=1, tiled=True)  7.39 us
    unnamed x13, local copies, waits for them, and re-layouts  6.82 us
    scatter x1, local copies, waits for them, and re-layouts, place_rows(): buffer = buffer.at[target].set(part_rows)  4.61 us
  transfers between devices with their start and end apart: 2, of which 1 were waited for; matrix products, arithmetic and copies ran while one was open for 27% of the time, Pallas kernels for 0%

commit v1 on v0

v1 whole, which is shorter than its diff:
```python
import functools
import math

import jax
import jax.numpy as jnp
from jax import lax
from jax.experimental import pallas as pl
from jax.experimental.pallas import tpu as pltpu
from jax.sharding import PartitionSpec as P

HD = 128
QPK = 8
UNIT = 128
CHUNK = 256
MESH = pl.DeviceIdType.MESH
NT = (((1,), (1,)), ((), ()))


def body(
    n, rows, depth, parts, kept, page, per_owner, slot_most, pool_dev,
    hidden_hbm, w_hbm, bias_ref, routes_ref, lists_ref, pool_hbm, out_hbm,
    hid, wv, biasv, acc, projv, place, send, recv, psend, precv, poolv,
    keys, vals, mask, alive, outv,
    hid_sem, w_sem, pool_sem, ps_sem, pr_sem, send_sem, recv_sem, out_sem,
):
    f32, bf16, i32 = jnp.float32, jnp.bfloat16, jnp.int32
    me = lax.axis_index("sess")
    head = lax.axis_index("tp")
    sessions = n * per_owner
    seg = n * slot_most
    hist = kept * page
    slots = sessions * slot_most
    chunks = (QPK + 2) * HD // CHUNK
    block = depth // parts

    barrier = pltpu.get_barrier_semaphore()

    def greet(k, carry):
        pl.semaphore_signal(
            barrier, inc=1, device_id={"sess": lax.rem(me + k, n)}, device_id_type=MESH
        )
        return carry

    lax.fori_loop(1, n, greet, 0)

    def pool_copy():
        return pltpu.make_async_copy(pool_hbm, poolv, pool_sem)

    def hid_copy(k):
        return pltpu.make_async_copy(
            hidden_hbm.at[:, pl.ds(k * block, block)], hid.at[k], hid_sem.at[k]
        )

    def w_copy(c, k):
        first = lax.rem(c + chunks - 1, chunks) * CHUNK
        return pltpu.make_async_copy(
            w_hbm.at[pl.ds(pl.multiple_of(k * block, block), block),
                     pl.ds(pl.multiple_of(first, CHUNK), CHUNK)],
            wv.at[c, k],
            w_sem.at[c, k],
        )

    pool_copy().start()
    for k in range(parts):
        hid_copy(k).start()
        w_copy(0, k).start()

    def fetch(i, carry):
        w_copy(1 + i // parts, i % parts).start()
        return carry

    lax.fori_loop(0, (chunks - 1) * parts, fetch, 0)

    pool_copy().wait()

    def pick(o, carry):
        chosen = jnp.int32(0)
        for l in range(per_owner):
            for k in range(kept):
                listed = lists_ref[head, k, o * per_owner + l]
                chosen = chosen + jnp.where(listed // pool_dev == me, listed % pool_dev, 0)
        psend[o] = poolv[chosen]
        return carry

    lax.fori_loop(0, n, pick, 0)
    precv[me] = psend[me]

    pl.semaphore_wait(barrier, n - 1)

    def page_copy(k):
        to = lax.rem(me + k, n)
        return pltpu.make_async_remote_copy(
            src_ref=psend.at[to], dst_ref=precv.at[me], send_sem=ps_sem, recv_sem=pr_sem,
            device_id={"sess": to}, device_id_type=MESH,
        )

    def send_page(k, carry):
        page_copy(k).start()
        return carry

    lax.fori_loop(1, n, send_page, 0)

    destination = routes_ref[pl.ds(me, 1), :]
    onehot = (lax.broadcasted_iota(i32, (sessions, rows), 0) == destination).astype(f32)
    earlier = (
        lax.broadcasted_iota(i32, (rows, rows), 0) < lax.broadcasted_iota(i32, (rows, rows), 1)
    ).astype(bf16)
    before = jnp.dot(onehot.astype(bf16), earlier, preferred_element_type=f32)
    ranking = jnp.sum(onehot * before, axis=0, keepdims=True)
    target = destination.astype(f32) * float(slot_most) + ranking
    steps = slots // CHUNK

    def fill(m, carry):
        ids = lax.broadcasted_iota(i32, (CHUNK, rows), 0) + m * CHUNK
        place[m] = (ids.astype(f32) == target).astype(bf16)
        return carry

    lax.fori_loop(0, steps, fill, 0)

    width = routes_ref.shape[0]
    for l in range(per_owner):
        same = (routes_ref[...] == me * per_owner + l).astype(f32)
        count_col = jnp.sum(same, axis=1, keepdims=True)
        count_row = lax.dot_general(
            jnp.ones((8, rows), bf16), same.astype(bf16), NT, preferred_element_type=f32
        )
        spread = (
            lax.broadcasted_iota(i32, (width, seg), 1) // slot_most
            == lax.broadcasted_iota(i32, (width, seg), 0)
        ).astype(bf16)
        spread_t = (
            lax.broadcasted_iota(i32, (seg, width), 0) // slot_most
            == lax.broadcasted_iota(i32, (seg, width), 1)
        ).astype(bf16)
        row_counts = jnp.dot(count_row.astype(bf16), spread, preferred_element_type=f32)
        col_counts = jnp.dot(
            spread_t, jnp.broadcast_to(count_col, (width, HD)).astype(bf16),
            preferred_element_type=f32,
        )
        row_off = (lax.broadcasted_iota(i32, (8, seg), 1) % slot_most).astype(f32)
        col_off = (lax.broadcasted_iota(i32, (seg, HD), 0) % slot_most).astype(f32)
        alive[l] = (col_off < col_counts).astype(f32)
        live_row = jnp.where(row_off < row_counts, 0.0, -1e30)[0:1, :]
        mask[l] = jnp.where(
            lax.broadcasted_iota(i32, (seg, seg), 1) <= lax.broadcasted_iota(i32, (seg, seg), 0),
            live_row, -1e30,
        )
        vals[l, :, HD:] = jnp.ones((hist + seg, HD), bf16)

    for c in range(chunks):
        first = ((c + chunks - 1) % chunks) * CHUNK
        biasv[c] = jnp.broadcast_to(bias_ref[0:1, first : first + CHUNK], (8, CHUNK))

    def row_copy(u, k):
        to = lax.rem(me + k, n)
        return pltpu.make_async_remote_copy(
            src_ref=send.at[u, pl.ds(to * per_owner, per_owner)],
            dst_ref=recv.at[u, :, pl.ds(pl.multiple_of(me * slot_most, slot_most), slot_most)],
            send_sem=send_sem.at[u], recv_sem=recv_sem.at[u],
            device_id={"sess": to}, device_id_type=MESH,
        )

    def project(c, carry):
        acc[...] = jnp.zeros_like(acc)

        def multiply(k, inner):
            @pl.when(c == 0)
            def _():
                hid_copy(k).wait()

            w_copy(c, k).wait()
            acc[...] += jnp.dot(hid[k], wv[c, k], preferred_element_type=f32)
            return inner

        lax.fori_loop(0, parts, multiply, 0)
        projv[...] = (acc[...] + biasv[c][0:1, :]).astype(bf16)

        def put(m, inner):
            placed = jnp.dot(place[m], projv[...], preferred_element_type=f32).astype(bf16)
            group = CHUNK // slot_most
            at = pl.ds(m * group, group)
            send[2 * c, at] = placed[:, :UNIT].reshape(group, slot_most, UNIT)
            send[2 * c + 1, at] = placed[:, UNIT:].reshape(group, slot_most, UNIT)
            return inner

        lax.fori_loop(0, steps, put, 0)

        def ship(k, inner):
            row_copy(2 * c, k).start()
            row_copy(2 * c + 1, k).start()
            return inner

        lax.fori_loop(1, n, ship, 0)
        own = pl.ds(pl.multiple_of(me * slot_most, slot_most), slot_most)
        for u in range(2):
            recv[2 * c + u, :, own, :] = send[2 * c + u, pl.ds(me * per_owner, per_owner)]
        return carry

    lax.fori_loop(0, chunks, project, 0)

    def arrived(u):
        part = recv.at[u, :, pl.ds(0, seg - slot_most)]
        pltpu.make_async_copy(part, part, recv_sem.at[u]).wait()

    part = precv.at[pl.ds(0, n - 1)]
    pltpu.make_async_copy(part, part, pr_sem).wait()
    for l in range(per_owner):
        for k in range(kept):
            source = lists_ref[head, k, me * per_owner + l] // pool_dev
            got = precv[source]
            keys[l, k * page : (k + 1) * page, :] = got[:, :HD]
            vals[l, k * page : (k + 1) * page, :HD] = got[:, HD:]
    arrived(0)
    arrived(1)
    for l in range(per_owner):
        keys[l, hist:, :] = recv[0, l]
        vals[l, hist:, :HD] = recv[1, l]

    tile = min(seg, 256)
    factor = math.log2(math.e) / math.sqrt(HD)

    def out_copy(h):
        return pltpu.make_async_copy(
            outv.at[h], out_hbm.at[:, :, pl.ds(pl.multiple_of(h * HD, HD), HD)], out_sem.at[h]
        )

    def attend(h, carry):
        arrived(2 + h)
        for l in range(per_owner):
            for start in range(0, seg, tile):
                upto = start + tile
                query = recv[2 + h, l, start:upto, :]
                past = lax.dot_general(query, keys[l, :hist, :], NT, preferred_element_type=f32)
                turn = lax.dot_general(
                    query, keys[l, hist : hist + upto, :], NT, preferred_element_type=f32
                )
                turn = turn + mask[l, start:upto, :upto]
                top = jnp.maximum(
                    jnp.max(past, axis=1, keepdims=True), jnp.max(turn, axis=1, keepdims=True)
                )
                past = jnp.exp2((past - top) * factor).astype(bf16)
                turn = jnp.exp2((turn - top) * factor).astype(bf16)
                total = jnp.dot(past, vals[l, :hist, :], preferred_element_type=f32)
                total += jnp.dot(turn, vals[l, hist : hist + upto, :], preferred_element_type=f32)
                mixed = total[:, :HD] / total[:, HD:]
                mixed = jnp.where(alive[l, start:upto, :] > 0.0, mixed, 0.0)
                outv[h, l, start:upto, :] = mixed.astype(bf16)
        out_copy(h).start()
        return carry

    lax.fori_loop(0, QPK, attend, 0)

    def finish(h, carry):
        out_copy(h).wait()
        return carry

    lax.fori_loop(0, QPK, finish, 0)
    part = psend.at[pl.ds(0, n - 1)]
    pltpu.make_async_copy(part, part, ps_sem).wait()

    def sent(u, carry):
        part = send.at[u, pl.ds(0, sessions - per_owner)]
        pltpu.make_async_copy(part, part, send_sem.at[u]).wait()
        return carry

    lax.fori_loop(0, 2 * chunks, sent, 0)


def on_device(hidden, routes, w_qkv, b_qkv, pool, page_lists):
    n = lax.axis_size("sess")
    rows, depth = hidden.shape
    sessions, _, kept = page_lists.shape
    per_owner = sessions // n
    slot_most = 2 * rows // sessions
    seg = n * slot_most
    pool_dev, _, page, pair = pool.shape
    hist = kept * page
    columns = (QPK + 2) * HD
    chunks = columns // CHUNK
    units = columns // UNIT
    parts = 8
    f32, bf16 = jnp.float32, jnp.bfloat16
    vmem, anywhere = pl.BlockSpec(memory_space=pltpu.VMEM), pl.BlockSpec(memory_space=pl.ANY)
    dma = pltpu.SemaphoreType.DMA
    return pl.pallas_call(
        functools.partial(
            body, n, rows, depth, parts, kept, page, per_owner, slot_most, pool_dev
        ),
        out_shape=jax.ShapeDtypeStruct((per_owner, seg, QPK * HD), bf16),
        in_specs=[
            anywhere, anywhere, vmem, vmem, pl.BlockSpec(memory_space=pltpu.SMEM), anywhere,
        ],
        out_specs=anywhere,
        scratch_shapes=[
            pltpu.VMEM((parts, rows, depth // parts), bf16),
            pltpu.VMEM((chunks, parts, depth // parts, CHUNK), bf16),
            pltpu.VMEM((chunks, 8, CHUNK), f32),
            pltpu.VMEM((rows, CHUNK), f32),
            pltpu.VMEM((rows, CHUNK), bf16),
            pltpu.VMEM((sessions * slot_most // CHUNK, CHUNK, rows), bf16),
            pltpu.VMEM((units, sessions, slot_most, UNIT), bf16),
            pltpu.VMEM((units, per_owner, seg, UNIT), bf16),
            pltpu.VMEM((n, page, pair), bf16),
            pltpu.VMEM((n, page, pair), bf16),
            pltpu.VMEM((pool_dev, page, pair), bf16),
            pltpu.VMEM((per_owner, hist + seg, HD), bf16),
            pltpu.VMEM((per_owner, hist + seg, 2 * HD), bf16),
            pltpu.VMEM((per_owner, seg, seg), f32),
            pltpu.VMEM((per_owner, seg, HD), f32),
            pltpu.VMEM((QPK, per_owner, seg, HD), bf16),
            dma((parts,)),
            dma((chunks, parts)),
            dma(()),
            dma(()),
            dma(()),
            dma((units,)),
            dma((units,)),
            dma((QPK,)),
        ],
        compiler_params=pltpu.CompilerParams(
            collective_id=0, has_side_effects=True, vmem_limit_bytes=62 * 2**20
        ),
        name="routed_attention",
    )(
        hidden,
        w_qkv[:, 0, :],
        b_qkv,
        routes.reshape(n, rows),
        jnp.transpose(page_lists, (1, 2, 0)),
        pool[:, 0],
    )


def solution(mesh):
    in_specs = (
        P("sess", None),
        P(),
        P(None, "tp", None),
        P("tp", None),
        P("sess", "tp", None, None),
        P(),
    )
    return jax.shard_map(
        on_device, mesh=mesh, in_specs=in_specs, out_specs=P("sess", None, "tp"), check_vma=False
    )
```

time: 130 us -> 69.8 us (0.54)
  Pallas kernels: 0 us -> 62.6 us
  matrix products: 51.6 us -> 0 us
  waiting for transfers between devices: 28.3 us -> 0 us
  local copies, waits for them, and re-layouts: 27.8 us -> 4.23 us
  starting transfers between devices: 16.9 us -> 0 us
  other arithmetic: 4.97 us -> 1.64 us
    pallas_call x0 -> x1, Pallas kernels: none -> 62.6 us  [on_device(): pl.pallas_call(functools.partial(body, n, rows, depth, parts, kept, page,...]
    dot_general x2 -> x0, matrix products: 29.7 us -> none  [the longest x1 17.6 us: on_device(): local_rows = jnp.dot(hidden, weights, preferred_element_type=jnp.float32)]
    all_to_all x2 -> x0, waiting for transfers between devices: 28.3 us -> none  [the longest x1 28.3 us: on_device(): lax.all_to_all(sendable, 'sess', split_axis=1, concat_axis=1, tiled=True)]
    sub x1 -> x0, matrix products: 21.9 us -> none  [on_device(): expo = jnp.where(allowed, jnp.exp(scores - top), 0.0)]
    all_to_all x2 -> x0, starting transfers between devices: 16.9 us -> none  [the longest x1 9.49 us: on_device(): lax.all_to_all(outgoing, 'sess', split_axis=0, concat_axis=0, tiled=True)]
    scatter x1 -> x0, local copies, waits for them, and re-layouts: 4.61 us -> none  [place_rows(): buffer = buffer.at[target].set(part_rows)]
    slice x4 -> x0, local copies, waits for them, and re-layouts: 4.14 us -> none  [the longest x1 2.76 us: on_device(): query = qkv[:, :, :query_cols].reshape(per_owner, segment, QPK, HD)]
    reshape x3 -> x1, local copies, waits for them, and re-layouts: 4.35 us -> 0.64 us  [on_device(): routes.reshape(n, rows)]
  transfers between devices with their start and end apart: 2 -> 0, of which waited for: 1 -> 0; matrix products, arithmetic and copies ran while one was open for 27% -> 0% of each run, Pallas kernels for 0% -> 0%
where the time goes in v1:
time: 69.8 us; the launch traced here: 68.5 us
  Pallas kernels  62.6 us (90%)
  local copies, waits for them, and re-layouts  4.23 us (6%)
  other arithmetic  1.64 us (2%)
    pallas_call x1, Pallas kernels, on_device(): pl.pallas_call(functools.partial(body, n, rows, depth, parts, kept, page,...  62.6 us
    unnamed x2, local copies, waits for them, and re-layouts  3.59 us
    unnamed x1, other arithmetic  1.64 us

profile of v1, /device:TPU:1, one launch (start us, length us, event | category | flops | bytes accessed | tf_op | source)
XLA Modules:
  0.0 68.5 jit_solution(17877269195476498617)
XLA Ops:
  0.0 0.5 broadcast.3
  0.5 1.6 %reduce.3 = s32[16384]{0:T(1024)S(1)} reduce(s32[16384,1]{0,1:T(1,128)} %param.7, s32[]{:T(128)} %broadcast.3), dimensions={1}, to_apply=%param.7.reduce_sub_computation.3 | reduce | bytes 131076 | tf_op args[1]
  2.2 0.6 reshape.3.routes_ref
  2.8 62.6 %routed_attention.1 = bf16[2,512,1024]{2,1,0:T(8,128)(2,1)} custom-call(bf16[512,8192]{1,0:T(8,128)(2,1)} %hidden_hbm.1, bf16[8192,1280]{1,0:T(8,128)(2,1)} %bitcast.4, f32[1,1280]{1,0:T(1,128)} %bias_ref.1, s32[32,512]{1,0:T(8,128)} %reshape.3.routes_ref, s32[4,8,64]{2,1,0:T(8,128)} %bitcast.6, bf16[16,64,256]{2,1,0:T(8,128)(2,1)} %bitcast.5), custom_call_target="tpu_custom_call" | custom-call | tf_op jit(solution)/shard_map/routed_attention/pallas_call | solution.py:285
  65.4 3.1 %copy.8 = bf16[2,512,1024]{2,1,0:T(8,128)(2,1)} copy(bf16[2,512,1024]{2,1,0:T(8,128)(2,1)} %routed_attention.1) | data formatting | bytes 4194304

commit v2 on v1

v2 whole, which is shorter than its diff:
```python
import functools
import math

import jax
import jax.numpy as jnp
from jax import lax
from jax.experimental import pallas as pl
from jax.experimental.pallas import tpu as pltpu
from jax.sharding import PartitionSpec as P

HD = 128
QPK = 8
UNIT = 128
CHUNK = 256
MESH = pl.DeviceIdType.MESH
NT = (((1,), (1,)), ((), ()))


def body(
    n, rows, depth, parts, kept, page, per_owner, slot_most, pool_dev,
    hidden_hbm, w_hbm, bias_ref, routes_ref, lists_ref, pool_hbm, out_ref,
    hid, wv, biasv, acc, projv, place, send, recv, psend, precv, poolv,
    keys, vals, mask, alive, blocks,
    hid_sem, w_sem, pool_sem, ps_sem, pr_sem, send_sem, recv_sem,
):
    f32, bf16, i32 = jnp.float32, jnp.bfloat16, jnp.int32
    me = lax.axis_index("sess")
    head = lax.axis_index("tp")
    sessions = n * per_owner
    seg = n * slot_most
    hist = kept * page
    slots = sessions * slot_most
    chunks = (QPK + 2) * HD // CHUNK
    block = depth // parts

    planes = n // 8
    mine_x, mine_z, mine_c = lax.div(me, 8), lax.rem(lax.div(me, 2), 4), lax.rem(me, 2)

    def peer(k):
        at_x = lax.rem(mine_x + lax.div(k, 8), planes)
        at_z = lax.rem(mine_z + lax.rem(lax.div(k, 2), 4), 4)
        return (at_x * 4 + at_z) * 2 + lax.rem(mine_c + lax.rem(k, 2), 2)

    barrier = pltpu.get_barrier_semaphore()

    def pool_copy():
        return pltpu.make_async_copy(pool_hbm, poolv, pool_sem)

    pool_copy().start()

    def greet(k, carry):
        pl.semaphore_signal(
            barrier, inc=1, device_id={"sess": peer(k)}, device_id_type=MESH
        )
        return carry

    lax.fori_loop(1, n, greet, 0)

    def hid_copy(k):
        return pltpu.make_async_copy(
            hidden_hbm.at[:, pl.ds(k * block, block)], hid.at[k], hid_sem.at[k]
        )

    def w_copy(c, k):
        first = lax.rem(c + chunks - 1, chunks) * CHUNK
        return pltpu.make_async_copy(
            w_hbm.at[pl.ds(pl.multiple_of(k * block, block), block),
                     pl.ds(pl.multiple_of(first, CHUNK), CHUNK)],
            wv.at[lax.rem(c, 2), k],
            w_sem.at[lax.rem(c, 2), k],
        )

    pool_copy().wait()
    for k in range(parts):
        hid_copy(k).start()
        w_copy(jnp.int32(0), k).start()

    pl.semaphore_wait(barrier, n - 1)

    def page_copy(k):
        to = peer(k)
        return pltpu.make_async_remote_copy(
            src_ref=psend.at[to], dst_ref=precv.at[me], send_sem=ps_sem, recv_sem=pr_sem,
            device_id={"sess": to}, device_id_type=MESH,
        )

    def pick(k, carry):
        o = peer(k)
        chosen = jnp.int32(0)
        for l in range(per_owner):
            for i in range(kept):
                slot = lists_ref[head, i, o * per_owner + l] - me * pool_dev
                chosen += jnp.where((slot >= 0) & (slot < pool_dev), slot, 0)
        psend[o] = poolv[chosen]

        @pl.when(k > 1)
        def _():
            page_copy(k - 1).start()

        return carry

    lax.fori_loop(1, n, pick, 0)
    pick(0, 0)
    page_copy(n - 1).start()
    precv[me] = psend[me]

    destination = routes_ref[:, pl.ds(pl.multiple_of(me * rows, rows), rows)]
    onehot = (lax.broadcasted_iota(i32, (sessions, rows), 0) == destination).astype(f32)
    earlier = (
        lax.broadcasted_iota(i32, (rows, rows), 0) < lax.broadcasted_iota(i32, (rows, rows), 1)
    ).astype(bf16)
    before = jnp.dot(onehot.astype(bf16), earlier, preferred_element_type=f32)
    ranking = jnp.sum(onehot * before, axis=0, keepdims=True)
    target = destination.astype(f32) * float(slot_most) + ranking
    steps = slots // CHUNK

    def fill(m, carry):
        ids = lax.broadcasted_iota(i32, (CHUNK, rows), 0) + m * CHUNK
        place[m] = (ids.astype(f32) == target).astype(bf16)
        return carry

    lax.fori_loop(0, steps, fill, 0)

    for c in range(chunks):
        first = ((c + chunks - 1) % chunks) * CHUNK
        biasv[c] = jnp.broadcast_to(bias_ref[0:1, first : first + CHUNK], (8, CHUNK))

    def row_copy(u, k):
        to = peer(k)
        return pltpu.make_async_remote_copy(
            src_ref=send.at[u, pl.ds(to * per_owner, per_owner)],
            dst_ref=recv.at[u, :, pl.ds(pl.multiple_of(me * slot_most, slot_most), slot_most)],
            send_sem=send_sem.at[u], recv_sem=recv_sem.at[u],
            device_id={"sess": to}, device_id_type=MESH,
        )

    def project(c, carry):
        acc[...] = jnp.zeros_like(acc)

        def multiply(k, inner):
            @pl.when(c == 0)
            def _():
                hid_copy(k).wait()

            w_copy(c, k).wait()

            @pl.when(c < chunks - 1)
            def _():
                w_copy(c + 1, k).start()

            acc[...] += jnp.dot(hid[k], wv[lax.rem(c, 2), k], preferred_element_type=f32)
            return inner

        lax.fori_loop(0, parts, multiply, 0)
        projv[...] = (acc[...] + biasv[c][0:1, :]).astype(bf16)

        def put(m, inner):
            placed = jnp.dot(place[m], projv[...], preferred_element_type=f32).astype(bf16)
            group = CHUNK // slot_most
            at = pl.ds(m * group, group)
            send[2 * c, at] = placed[:, :UNIT].reshape(group, slot_most, UNIT)
            send[2 * c + 1, at] = placed[:, UNIT:].reshape(group, slot_most, UNIT)
            return inner

        lax.fori_loop(0, steps, put, 0)

        def ship(k, inner):
            row_copy(2 * c, k).start()
            row_copy(2 * c + 1, k).start()
            return inner

        lax.fori_loop(1, n, ship, 0)
        own = pl.ds(pl.multiple_of(me * slot_most, slot_most), slot_most)
        for u in range(2):
            recv[2 * c + u, :, own, :] = send[2 * c + u, pl.ds(me * per_owner, per_owner)]
        return carry

    lax.fori_loop(0, chunks, project, 0)

    def arrived(u):
        part = recv.at[u, :, pl.ds(0, seg - slot_most)]
        pltpu.make_async_copy(part, part, recv_sem.at[u]).wait()

    for b in range(n):
        blocks[b : b + 1, :] = routes_ref[:, b * rows : (b + 1) * rows]
    for l in range(per_owner):
        same = (blocks[...] == me * per_owner + l).astype(f32)
        count_col = jnp.sum(same, axis=1, keepdims=True)
        count_row = lax.dot_general(
            jnp.ones((8, rows), bf16), same.astype(bf16), NT, preferred_element_type=f32
        )
        spread = (
            lax.broadcasted_iota(i32, (n, seg), 1) // slot_most
            == lax.broadcasted_iota(i32, (n, seg), 0)
        ).astype(bf16)
        spread_t = (
            lax.broadcasted_iota(i32, (seg, n), 0) // slot_most
            == lax.broadcasted_iota(i32, (seg, n), 1)
        ).astype(bf16)
        row_counts = jnp.dot(count_row.astype(bf16), spread, preferred_element_type=f32)
        col_counts = jnp.dot(
            spread_t, jnp.broadcast_to(count_col, (n, HD)).astype(bf16),
            preferred_element_type=f32,
        )
        row_off = (lax.broadcasted_iota(i32, (8, seg), 1) % slot_most).astype(f32)
        col_off = (lax.broadcasted_iota(i32, (seg, HD), 0) % slot_most).astype(f32)
        alive[l] = (col_off < col_counts).astype(f32)
        live_row = jnp.where(row_off < row_counts, 0.0, -1e30)[0:1, :]
        mask[l] = jnp.where(
            lax.broadcasted_iota(i32, (seg, seg), 1) <= lax.broadcasted_iota(i32, (seg, seg), 0),
            live_row, -1e30,
        )
        vals[l, :, HD:] = jnp.ones((hist + seg, HD), bf16)

    part = precv.at[pl.ds(0, n - 1)]
    pltpu.make_async_copy(part, part, pr_sem).wait()
    for l in range(per_owner):
        for k in range(kept):
            source = lists_ref[head, k, me * per_owner + l] // pool_dev
            got = precv[source]
            keys[l, k * page : (k + 1) * page, :] = got[:, :HD]
            vals[l, k * page : (k + 1) * page, :HD] = got[:, HD:]
    arrived(0)
    arrived(1)
    for l in range(per_owner):
        keys[l, hist:, :] = recv[0, l]
        vals[l, hist:, :HD] = recv[1, l]

    tile = min(seg, 256)
    factor = math.log2(math.e) / math.sqrt(HD)

    def attend(h, carry):
        arrived(2 + h)
        for l in range(per_owner):
            for start in range(0, seg, tile):
                upto = start + tile
                query = recv[2 + h, l, start:upto, :]
                past = lax.dot_general(query, keys[l, :hist, :], NT, preferred_element_type=f32)
                turn = lax.dot_general(
                    query, keys[l, hist : hist + upto, :], NT, preferred_element_type=f32
                )
                turn = turn + mask[l, start:upto, :upto]
                top = jnp.maximum(
                    jnp.max(past, axis=1, keepdims=True), jnp.max(turn, axis=1, keepdims=True)
                )
                past = jnp.exp2((past - top) * factor).astype(bf16)
                turn = jnp.exp2((turn - top) * factor).astype(bf16)
                total = jnp.dot(past, vals[l, :hist, :], preferred_element_type=f32)
                total += jnp.dot(turn, vals[l, hist : hist + upto, :], preferred_element_type=f32)
                mixed = total[:, :HD] / total[:, HD:]
                mixed = jnp.where(alive[l, start:upto, :] > 0.0, mixed, 0.0)
                out_ref[l, start:upto, pl.ds(pl.multiple_of(h * HD, HD), HD)] = mixed.astype(bf16)
        return carry

    lax.fori_loop(0, QPK, attend, 0)

    part = psend.at[pl.ds(0, n - 1)]
    pltpu.make_async_copy(part, part, ps_sem).wait()

    def sent(u, carry):
        part = send.at[u, pl.ds(0, sessions - per_owner)]
        pltpu.make_async_copy(part, part, send_sem.at[u]).wait()
        return carry

    lax.fori_loop(0, 2 * chunks, sent, 0)


def on_device(hidden, routes, w_qkv, b_qkv, pool, page_lists):
    n = lax.axis_size("sess")
    rows, depth = hidden.shape
    sessions, _, kept = page_lists.shape
    per_owner = sessions // n
    slot_most = 2 * rows // sessions
    seg = n * slot_most
    pool_dev, _, page, pair = pool.shape
    hist = kept * page
    columns = (QPK + 2) * HD
    chunks = columns // CHUNK
    units = columns // UNIT
    parts = 8
    f32, bf16 = jnp.float32, jnp.bfloat16
    vmem, anywhere = pl.BlockSpec(memory_space=pltpu.VMEM), pl.BlockSpec(memory_space=pl.ANY)
    dma = pltpu.SemaphoreType.DMA
    return pl.pallas_call(
        functools.partial(
            body, n, rows, depth, parts, kept, page, per_owner, slot_most, pool_dev
        ),
        out_shape=jax.ShapeDtypeStruct((per_owner, seg, QPK * HD), bf16),
        in_specs=[
            anywhere, anywhere, vmem, vmem, pl.BlockSpec(memory_space=pltpu.SMEM), anywhere,
        ],
        out_specs=vmem,
        scratch_shapes=[
            pltpu.VMEM((parts, rows, depth // parts), bf16),
            pltpu.VMEM((2, parts, depth // parts, CHUNK), bf16),
            pltpu.VMEM((chunks, 8, CHUNK), f32),
            pltpu.VMEM((rows, CHUNK), f32),
            pltpu.VMEM((rows, CHUNK), bf16),
            pltpu.VMEM((sessions * slot_most // CHUNK, CHUNK, rows), bf16),
            pltpu.VMEM((units, sessions, slot_most, UNIT), bf16),
            pltpu.VMEM((units, per_owner, seg, UNIT), bf16),
            pltpu.VMEM((n, page, pair), bf16),
            pltpu.VMEM((n, page, pair), bf16),
            pltpu.VMEM((pool_dev, page, pair), bf16),
            pltpu.VMEM((per_owner, hist + seg, HD), bf16),
            pltpu.VMEM((per_owner, hist + seg, 2 * HD), bf16),
            pltpu.VMEM((per_owner, seg, seg), f32),
            pltpu.VMEM((per_owner, seg, HD), f32),
            pltpu.VMEM((n, rows), jnp.int32),
            dma((parts,)),
            dma((2, parts)),
            dma(()),
            dma(()),
            dma(()),
            dma((units,)),
            dma((units,)),
        ],
        compiler_params=pltpu.CompilerParams(
            collective_id=0, has_side_effects=True, vmem_limit_bytes=48 * 2**20
        ),
        name="routed_attention",
    )(
        hidden,
        w_qkv[:, 0, :],
        b_qkv,
        routes.T,
        jnp.transpose(page_lists, (1, 2, 0)),
        pool[:, 0],
    )


def solution(mesh):
    in_specs = (
        P("sess", None),
        P(),
        P(None, "tp", None),
        P("tp", None),
        P("sess", "tp", None, None),
        P(),
    )
    return jax.shard_map(
        on_device, mesh=mesh, in_specs=in_specs, out_specs=P("sess", None, "tp"), check_vma=False
    )
```

time: 69.8 us -> 62.6 us (0.90); the launches traced: 68.5 us -> 62.3 us
  Pallas kernels: 62.6 us -> 57.7 us
  other arithmetic: 1.64 us -> 0 us
    pallas_call x1, Pallas kernels: 62.6 us -> 57.7 us  [on_device(): pl.pallas_call(functools.partial(body, n, rows, depth, parts, kept, page,...]
    unnamed x1 -> x0, other arithmetic: 1.64 us -> none
    unnamed x2 -> x9, local copies, waits for them, and re-layouts: 3.59 us -> 4.61 us
where the time goes in v2:
time: 62.6 us; the launch traced here: 62.3 us
  Pallas kernels  57.7 us (92%)
  local copies, waits for them, and re-layouts  4.61 us (7%)
    pallas_call x1, Pallas kernels, on_device(): pl.pallas_call(functools.partial(body, n, rows, depth, parts, kept, page,...  57.7 us
    unnamed x9, local copies, waits for them, and re-layouts  4.61 us

profile of v2, /device:TPU:1, one launch (start us, length us, event | category | flops | bytes accessed | tf_op | source)
XLA Modules:
  0.0 62.3 jit_solution(2028450586454104897)
XLA Ops:
  0.0 0.0 copy-start
  0.0 1.0 %copy-done = bf16[16,1,64,256]{3,2,1,0:T(8,128)(2,1)S(1)} copy-done((bf16[16,1,64,256]{3,2,1,0:T(8,128)(2,1)S(1)}, bf16[16,1,64,256]{3,2,1,0:T(8,128)(2,1)}, u32[]{:S(2)}) %copy-start) | copy-done | bytes 524312
  1.0 0.0 copy-start.1
  1.0 0.8 %copy-done.1 = s32[16384,1]{0,1:T(1,128)S(1)} copy-done((s32[16384,1]{0,1:T(1,128)S(1)}, s32[16384,1]{0,1:T(1,128)}, u32[]{:S(2)}) %copy-start.1) | copy-done | bytes 65560
  1.9 0.0 copy-start.2
  1.9 0.7 %copy-done.2 = s32[64,4,8]{0,2,1:T(8,128)S(1)} copy-done((s32[64,4,8]{0,2,1:T(8,128)S(1)}, s32[64,4,8]{0,2,1:T(8,128)}, u32[]{:S(2)}) %copy-start.2) | copy-done | bytes 8216
  2.6 0.0 copy-start.3
  2.6 0.7 %copy-done.3 = f32[1,1280]{1,0:T(1,128)S(1)} copy-done((f32[1,1280]{1,0:T(1,128)S(1)}, f32[1,1280]{1,0:T(1,128)}, u32[]{:S(2)}) %copy-start.3) | copy-done | bytes 5144
  3.3 57.7 %routed_attention.1 = bf16[2,512,1024]{2,1,0:T(8,128)(2,1)S(1)} custom-call(bf16[512,8192]{1,0:T(8,128)(2,1)} %hidden_hbm.1, bf16[8192,1280]{1,0:T(8,128)(2,1)} %bitcast.7, f32[1,1280]{1,0:T(1,128)S(1)} %copy-done.3, s32[1,16384]{1,0:T(1,128)S(1)} %bitcast.5, s32[4,8,64]{2,1,0:T(8,128)S(1)} %bitcast.6, bf16[16,64,256]{2,1,0:T(8,128)(2,1)S(1)} %bitcast.4), custom_call_target="tpu_custom_call" | custom-call | tf_op jit(solution)/shard_map/routed_attention/pallas_call | solution.py:284
  61.0 1.3 %copy.8 = bf16[2,512,1024]{2,1,0:T(8,128)(2,1)} copy(bf16[2,512,1024]{2,1,0:T(8,128)(2,1)S(1)} %routed_attention.1) | data formatting | bytes 4194304
Async XLA Ops:
  0.0 1.0 %copy-start = (bf16[16,1,64,256]{3,2,1,0:T(8,128)(2,1)S(1)}, bf16[16,1,64,256]{3,2,1,0:T(8,128)(2,1)}, u32[]{:S(2)}) copy-start(bf16[16,1,64,256]{3,2,1,0:T(8,128)(2,1)} %param.10) | copy-start | bytes 1572868
  1.0 0.8 %copy-start.1 = (s32[16384,1]{0,1:T(1,128)S(1)}, s32[16384,1]{0,1:T(1,128)}, u32[]{:S(2)}) copy-start(s32[16384,1]{0,1:T(1,128)} %param.7) | copy-start | bytes 196612
  1.9 0.7 %copy-start.2 = (s32[64,4,8]{0,2,1:T(8,128)S(1)}, s32[64,4,8]{0,2,1:T(8,128)}, u32[]{:S(2)}) copy-start(s32[64,4,8]{0,2,1:T(8,128)} %param.11) | copy-start | bytes 24580
  2.6 0.7 %copy-start.3 = (f32[1,1280]{1,0:T(1,128)S(1)}, f32[1,1280]{1,0:T(1,128)}, u32[]{:S(2)}) copy-start(f32[1,1280]{1,0:T(1,128)} %bias_ref.1) | copy-start | bytes 15364

commit v3 on v2

--- a/solution.py
+++ b/solution.py
@@ -10,7 +10,6 @@
 
 HD = 128
 QPK = 8
-UNIT = 128
 CHUNK = 256
 MESH = pl.DeviceIdType.MESH
 NT = (((1,), (1,)), ((), ()))
@@ -18,10 +17,10 @@
 
 def body(
     n, rows, depth, parts, kept, page, per_owner, slot_most, pool_dev,
-    hidden_hbm, w_hbm, bias_ref, routes_ref, lists_ref, pool_hbm, out_ref,
+    hidden_hbm, w_hbm, bias_hbm, routes_hbm, lists_hbm, pool_hbm, out_ref,
     hid, wv, biasv, acc, projv, place, send, recv, psend, precv, poolv,
-    keys, vals, mask, alive, blocks,
-    hid_sem, w_sem, pool_sem, ps_sem, pr_sem, send_sem, recv_sem,
+    keys, vals, mask, alive, blocks, bias_ref, routes_ref, lists_ref,
+    hid_sem, w_sem, small_sem, ps_sem, pr_sem, send_sem, recv_sem,
 ):
     f32, bf16, i32 = jnp.float32, jnp.bfloat16, jnp.int32
     me = lax.axis_index("sess")
@@ -35,26 +34,26 @@
 
     planes = n // 8
     mine_x, mine_z, mine_c = lax.div(me, 8), lax.rem(lax.div(me, 2), 4), lax.rem(me, 2)
-
-    def peer(k):
-        at_x = lax.rem(mine_x + lax.div(k, 8), planes)
-        at_z = lax.rem(mine_z + lax.rem(lax.div(k, 2), 4), 4)
-        return (at_x * 4 + at_z) * 2 + lax.rem(mine_c + lax.rem(k, 2), 2)
+    at_x = [lax.rem(mine_x + d, planes) * 8 for d in range(planes)]
+    at_z = [lax.rem(mine_z + d, 4) * 2 for d in range(4)]
+    at_c = [mine_c, 1 - mine_c]
+    offsets = [(x, z, c) for x in range(planes) for z in range(4) for c in range(2)][1:]
+    offsets.sort(key=lambda o: (o[2],o[0],o[1]), reverse=True)
+    peers = [at_x[x] + at_z[z] + at_c[c] for x, z, c in offsets]
 
     barrier = pltpu.get_barrier_semaphore()
 
-    def pool_copy():
-        return pltpu.make_async_copy(pool_hbm, poolv, pool_sem)
-
-    pool_copy().start()
-
-    def greet(k, carry):
-        pl.semaphore_signal(
-            barrier, inc=1, device_id={"sess": peer(k)}, device_id_type=MESH
-        )
-        return carry
-
-    lax.fori_loop(1, n, greet, 0)
+    small = [
+        pltpu.make_async_copy(pool_hbm, poolv, small_sem.at[0]),
+        pltpu.make_async_copy(lists_hbm.at[head], lists_ref, small_sem.at[1]),
+        pltpu.make_async_copy(routes_hbm, routes_ref, small_sem.at[2]),
+        pltpu.make_async_copy(bias_hbm, bias_ref, small_sem.at[3]),
+    ]
+    for copy in small:
+        copy.start()
+
+    for to in peers:
+        pl.semaphore_signal(barrier, inc=1, device_id={"sess": to}, device_id_type=MESH)
 
     def hid_copy(k):
         return pltpu.make_async_copy(
@@ -70,38 +69,31 @@
             w_sem.at[lax.rem(c, 2), k],
         )
 
-    pool_copy().wait()
+    for copy in small:
+        copy.wait()
     for k in range(parts):
         hid_copy(k).start()
         w_copy(jnp.int32(0), k).start()
 
     pl.semaphore_wait(barrier, n - 1)
 
-    def page_copy(k):
-        to = peer(k)
+    def page_copy(to):
         return pltpu.make_async_remote_copy(
             src_ref=psend.at[to], dst_ref=precv.at[me], send_sem=ps_sem, recv_sem=pr_sem,
             device_id={"sess": to}, device_id_type=MESH,
         )
 
-    def pick(k, carry):
-        o = peer(k)
+    picked = None
+    for o in peers + [me]:
         chosen = jnp.int32(0)
         for l in range(per_owner):
             for i in range(kept):
-                slot = lists_ref[head, i, o * per_owner + l] - me * pool_dev
+                slot = lists_ref[i, o * per_owner + l] - me * pool_dev
                 chosen += jnp.where((slot >= 0) & (slot < pool_dev), slot, 0)
         psend[o] = poolv[chosen]
-
-        @pl.when(k > 1)
-        def _():
-            page_copy(k - 1).start()
-
-        return carry
-
-    lax.fori_loop(1, n, pick, 0)
-    pick(0, 0)
-    page_copy(n - 1).start()
+        if picked is not None:
+            page_copy(picked).start()
+        picked = o
     precv[me] = psend[me]
 
     destination = routes_ref[:, pl.ds(pl.multiple_of(me * rows, rows), rows)]
@@ -125,12 +117,12 @@
         first = ((c + chunks - 1) % chunks) * CHUNK
         biasv[c] = jnp.broadcast_to(bias_ref[0:1, first : first + CHUNK], (8, CHUNK))
 
-    def row_copy(u, k):
-        to = peer(k)
+    def row_copy(c, to, columns, sem):
+        here = pl.ds(pl.multiple_of(me * slot_most, slot_most), slot_most)
         return pltpu.make_async_remote_copy(
-            src_ref=send.at[u, pl.ds(to * per_owner, per_owner)],
-            dst_ref=recv.at[u, :, pl.ds(pl.multiple_of(me * slot_most, slot_most), slot_most)],
-            send_sem=send_sem.at[u], recv_sem=recv_sem.at[u],
+            src_ref=send.at[c, pl.ds(to * per_owner, per_owner), :, columns],
+            dst_ref=recv.at[c, :, here, columns],
+            send_sem=send_sem.at[sem], recv_sem=recv_sem.at[sem],
             device_id={"sess": to}, device_id_type=MESH,
         )
 
@@ -158,21 +150,24 @@
             placed = jnp.dot(place[m], projv[...], preferred_element_type=f32).astype(bf16)
             group = CHUNK // slot_most
             at = pl.ds(m * group, group)
-            send[2 * c, at] = placed[:, :UNIT].reshape(group, slot_most, UNIT)
-            send[2 * c + 1, at] = placed[:, UNIT:].reshape(group, slot_most, UNIT)
+            send[c, at] = placed.reshape(group, slot_most, CHUNK)
             return inner
 
         lax.fori_loop(0, steps, put, 0)
 
-        def ship(k, inner):
-            row_copy(2 * c, k).start()
-            row_copy(2 * c + 1, k).start()
-            return inner
-
-        lax.fori_loop(1, n, ship, 0)
+        @pl.when(c < chunks - 1)
+        def _():
+            for to in peers:
+                row_copy(c, to, pl.ds(0, CHUNK), c).start()
+
+        @pl.when(c == chunks - 1)
+        def _():
+            for half in range(2):
+                for to in peers:
+                    row_copy(c, to, pl.ds(half * HD, HD), chunks - 1 + half).start()
+
         own = pl.ds(pl.multiple_of(me * slot_most, slot_most), slot_most)
-        for u in range(2):
-            recv[2 * c + u, :, own, :] = send[2 * c + u, pl.ds(me * per_owner, per_owner)]
+        recv[c, :, own, :] = send[c, pl.ds(me * per_owner, per_owner)]
         return carry
 
     lax.fori_loop(0, chunks, project, 0)
@@ -216,25 +211,33 @@
     pltpu.make_async_copy(part, part, pr_sem).wait()
     for l in range(per_owner):
         for k in range(kept):
-            source = lists_ref[head, k, me * per_owner + l] // pool_dev
+            source = lists_ref[k, me * per_owner + l] // pool_dev
             got = precv[source]
             keys[l, k * page : (k + 1) * page, :] = got[:, :HD]
             vals[l, k * page : (k + 1) * page, :HD] = got[:, HD:]
     arrived(0)
-    arrived(1)
     for l in range(per_owner):
-        keys[l, hist:, :] = recv[0, l]
-        vals[l, hist:, :HD] = recv[1, l]
+        keys[l, hist:, :] = recv[0, l, :, :HD]
+        vals[l, hist:, :HD] = recv[0, l, :, HD:]
 
     tile = min(seg, 256)
     factor = math.log2(math.e) / math.sqrt(HD)
 
     def attend(h, carry):
-        arrived(2 + h)
+        @pl.when((lax.rem(h, 2) == 0) & (h < QPK - 2))
+        def _():
+            arrived(1 + lax.div(h, 2))
+
+        @pl.when(h >= QPK - 2)
+        def _():
+            part = recv.at[chunks - 1, :, pl.ds(0, seg - slot_most), pl.ds(0, HD)]
+            pltpu.make_async_copy(part, part, recv_sem.at[chunks - 1 + h - (QPK - 2)]).wait()
+
+        half = pl.ds(pl.multiple_of(lax.rem(h, 2) * HD, HD), HD)
         for l in range(per_owner):
             for start in range(0, seg, tile):
                 upto = start + tile
-                query = recv[2 + h, l, start:upto, :]
+                query = recv[1 + lax.div(h, 2), l, start:upto, half]
                 past = lax.dot_general(query, keys[l, :hist, :], NT, preferred_element_type=f32)
                 turn = lax.dot_general(
                     query, keys[l, hist : hist + upto, :], NT, preferred_element_type=f32
@@ -262,7 +265,10 @@
         pltpu.make_async_copy(part, part, send_sem.at[u]).wait()
         return carry
 
-    lax.fori_loop(0, 2 * chunks, sent, 0)
+    lax.fori_loop(0, chunks - 1, sent, 0)
+    part = send.at[chunks - 1, pl.ds(0, sessions - per_owner), :, pl.ds(0, HD)]
+    for half in range(2):
+        pltpu.make_async_copy(part, part, send_sem.at[chunks - 1 + half]).wait()
 
 
 def on_device(hidden, routes, w_qkv, b_qkv, pool, page_lists):
@@ -276,19 +282,16 @@
     hist = kept * page
     columns = (QPK + 2) * HD
     chunks = columns // CHUNK
-    units = columns // UNIT
     parts = 8
     f32, bf16 = jnp.float32, jnp.bfloat16
-    vmem, anywhere = pl.BlockSpec(memory_space=pltpu.VMEM), pl.BlockSpec(memory_space=pl.ANY)
+    vmem, hbm = pl.BlockSpec(memory_space=pltpu.VMEM), pl.BlockSpec(memory_space=pltpu.HBM)
     dma = pltpu.SemaphoreType.DMA
     return pl.pallas_call(
         functools.partial(
             body, n, rows, depth, parts, kept, page, per_owner, slot_most, pool_dev
         ),
         out_shape=jax.ShapeDtypeStruct((per_owner, seg, QPK * HD), bf16),
-        in_specs=[
-            anywhere, anywhere, vmem, vmem, pl.BlockSpec(memory_space=pltpu.SMEM), anywhere,
-        ],
+        in_specs=[hbm] * 6,
         out_specs=vmem,
         scratch_shapes=[
             pltpu.VMEM((parts, rows, depth // parts), bf16),
@@ -297,8 +300,8 @@
             pltpu.VMEM((rows, CHUNK), f32),
             pltpu.VMEM((rows, CHUNK), bf16),
             pltpu.VMEM((sessions * slot_most // CHUNK, CHUNK, rows), bf16),
-            pltpu.VMEM((units, sessions, slot_most, UNIT), bf16),
-            pltpu.VMEM((units, per_owner, seg, UNIT), bf16),
+            pltpu.VMEM((chunks, sessions, slot_most, CHUNK), bf16),
+            pltpu.VMEM((chunks, per_owner, seg, CHUNK), bf16),
             pltpu.VMEM((n, page, pair), bf16),
             pltpu.VMEM((n, page, pair), bf16),
             pltpu.VMEM((pool_dev, page, pair), bf16),
@@ -307,25 +310,33 @@
             pltpu.VMEM((per_owner, seg, seg), f32),
             pltpu.VMEM((per_owner, seg, HD), f32),
             pltpu.VMEM((n, rows), jnp.int32),
+            pltpu.VMEM((1, columns), f32),
+            pltpu.VMEM((1, n * rows), jnp.int32),
+            pltpu.SMEM((kept, sessions), jnp.int32),
             dma((parts,)),
             dma((2, parts)),
+            dma((4,)),
             dma(()),
             dma(()),
-            dma(()),
-            dma((units,)),
-            dma((units,)),
+            dma((chunks + 1,)),
+            dma((chunks + 1,)),
         ],
         compiler_params=pltpu.CompilerParams(
             collective_id=0, has_side_effects=True, vmem_limit_bytes=48 * 2**20
         ),
         name="routed_attention",
     )(
-        hidden,
-        w_qkv[:, 0, :],
-        b_qkv,
-        routes.T,
-        jnp.transpose(page_lists, (1, 2, 0)),
-        pool[:, 0],
+        *[
+            pltpu.with_memory_space_constraint(array, pltpu.HBM)
+            for array in (
+                hidden,
+                w_qkv[:, 0, :],
+                b_qkv,
+                routes.T,
+                jnp.transpose(page_lists, (1, 2, 0)),
+                pool[:, 0],
+            )
+        ]
     )
 
 

time: 62.6 us -> 53.2 us (0.85)
  Pallas kernels: 57.7 us -> 51.8 us
  local copies, waits for them, and re-layouts: 4.61 us -> 1.32 us
    pallas_call x1, Pallas kernels: 57.7 us -> 51.8 us  [on_device(): pl.pallas_call(functools.partial(body, n, rows, depth, parts, kept, page,...]
    unnamed x9 -> x1, local copies, waits for them, and re-layouts: 4.61 us -> 1.32 us
where the time goes in v3:
time: 53.2 us; the launch traced here: 53.1 us
  Pallas kernels  51.8 us (97%)
  local copies, waits for them, and re-layouts  1.32 us (2%)
    pallas_call x1, Pallas kernels, on_device(): pl.pallas_call(functools.partial(body, n, rows, depth, parts, kept, page,...  51.8 us
    unnamed x1, local copies, waits for them, and re-layouts  1.32 us

profile of v3, /device:TPU:1, one launch (start us, length us, event | category | flops | bytes accessed | tf_op | source)
XLA Modules:
  0.0 53.1 jit_solution(3790764937866239145)
XLA Ops:
  0.0 51.8 %routed_attention.1 = bf16[2,512,1024]{2,1,0:T(8,128)(2,1)S(1)} custom-call(bf16[512,8192]{1,0:T(8,128)(2,1)} %hidden_hbm.1, bf16[8192,1280]{1,0:T(8,128)(2,1)} %bitcast.4, f32[1,1280]{1,0:T(1,128)} %bias_hbm.1, s32[1,16384]{1,0:T(1,128)} %bitcast.6, s32[4,8,64]{2,1,0:T(8,128)} %bitcast.7, bf16[16,64,256]{2,1,0:T(8,128)(2,1)} %bitcast.5), custom_call_target="tpu_custom_call" | custom-call | tf_op jit(solution)/shard_map/routed_attention/pallas_call | solution.py:289
  51.8 1.3 %copy.8 = bf16[2,512,1024]{2,1,0:T(8,128)(2,1)} copy(bf16[2,512,1024]{2,1,0:T(8,128)(2,1)S(1)} %routed_attention.1) | data formatting | bytes 4194304

commit v4 on v3

--- a/solution.py
+++ b/solution.py
@@ -49,11 +49,12 @@
         pltpu.make_async_copy(routes_hbm, routes_ref, small_sem.at[2]),
         pltpu.make_async_copy(bias_hbm, bias_ref, small_sem.at[3]),
     ]
+
+    for to in peers:
+        pl.semaphore_signal(barrier, inc=1, device_id={"sess": to}, device_id_type=MESH)
+
     for copy in small:
         copy.start()
-
-    for to in peers:
-        pl.semaphore_signal(barrier, inc=1, device_id={"sess": to}, device_id_type=MESH)
 
     def hid_copy(k):
         return pltpu.make_async_copy(

time: 53.2 us -> 53.2 us (level)
  no operation moved by 1% of the time
where the time goes in v4:
time: 53.2 us; the launch traced here: 53.1 us
  Pallas kernels  51.8 us (97%)
  local copies, waits for them, and re-layouts  1.32 us (2%)
    pallas_call x1, Pallas kernels, on_device(): pl.pallas_call(functools.partial(body, n, rows, depth, parts, kept, page,...  51.8 us
    unnamed x1, local copies, waits for them, and re-layouts  1.32 us

profile of v4, /device:TPU:1, one launch (start us, length us, event | category | flops | bytes accessed | tf_op | source)
XLA Modules:
  0.0 53.1 jit_solution(7149530702331496480)
XLA Ops:
  0.0 51.8 %routed_attention.1 = bf16[2,512,1024]{2,1,0:T(8,128)(2,1)S(1)} custom-call(bf16[512,8192]{1,0:T(8,128)(2,1)} %hidden_hbm.1, bf16[8192,1280]{1,0:T(8,128)(2,1)} %bitcast.4, f32[1,1280]{1,0:T(1,128)} %bias_hbm.1, s32[1,16384]{1,0:T(1,128)} %bitcast.6, s32[4,8,64]{2,1,0:T(8,128)} %bitcast.7, bf16[16,64,256]{2,1,0:T(8,128)(2,1)} %bitcast.5), custom_call_target="tpu_custom_call" | custom-call | tf_op jit(solution)/shard_map/routed_attention/pallas_call | solution.py:290
  51.8 1.3 %copy.8 = bf16[2,512,1024]{2,1,0:T(8,128)(2,1)} copy(bf16[2,512,1024]{2,1,0:T(8,128)(2,1)S(1)} %routed_attention.1) | data formatting | bytes 4194304
